TPU v7x, 256 devices: a whole 4x4x8 slice. The times are simulated.
256 devices in a mesh: ctx: 64 (over x, z, y_hi), tp: 4 (over y_lo, core).
Axes of the slice: x: 4, y: 4 (y_hi: 2, y_lo: 2; y = y_hi * 2 + y_lo), z: 8, core: 2. Of those that a mesh axis runs over, the one named last changes fastest.
Arguments:
- tokens: bfloat16 [16384, 8192], P('ctx'), may hold values from -6 to 6
- select_index: int32 [2048], P('ctx'), may hold values from 0 to 255, as said below
- valid_count: int32 [64], replicated, may hold values from 4 to 32, as said below
- queries: bfloat16 [2048, 4096], P('ctx', 'tp'), may hold values from -160 to 160
- key_matrix: bfloat16 [8192, 512], P('ctx', 'tp'), may hold values from -0.0625 to 0.0625
- value_matrix: bfloat16 [8192, 512], P('ctx', 'tp'), may hold values from -0.0625 to 0.0625
- out_grad: bfloat16 [2048, 4096], P('ctx', 'tp'), may hold values from -6 to 6
Outputs:
- attended: bfloat16 [2048, 4096], P('ctx', 'tp')
- query_gradient: bfloat16 [2048, 4096], P('ctx', 'tp')
- token_grad: bfloat16 [16384, 8192], P('ctx', 'tp')
- key_weight_grad: bfloat16 [8192, 512], P('ctx', 'tp')
- value_weight_grad: bfloat16 [8192, 512], P('ctx', 'tp')
Inputs may be any that keep to these rules, and one draw needn't show every extreme that they name: `select_index`: within one shard the offsets of all 32 slots are distinct, and those of the first valid_count slots rise. `valid_count`: some shard holds exactly 32 live slots.
All inputs are finite; a program needn't handle non-finite values.
Results may differ from a plain program's by a relative error of at most 0.023.
The roundings to bfloat16 on the way count: a program that leaves them out, or rounds other values in their place, can miss the bound.
Values may be sent and summed in bfloat16 or wider, within the bound.
A program may use at most 64 MiB of HBM per device.

v0:
```python
import math
import jax
import jax.numpy as jnp
from jax import lax
from jax.sharding import PartitionSpec as P

HEAD_WIDTH = 128
neg_large = -1e30


def local(tokens, select_index, valid_count, queries, key_matrix, value_matrix, out_grad):
    shard_len = tokens.shape[0]
    capacity = select_index.shape[0]
    key_value_width = key_matrix.shape[1]
    kv_local = key_value_width // HEAD_WIDTH
    per_group = queries.shape[1] // key_value_width
    ctx_size = lax.axis_size("ctx")
    own_shard = lax.axis_index("ctx")
    all_keys = ctx_size * capacity
    block_len = min(512, all_keys)
    num_blocks = all_keys // block_len
    score_scale = 1.0 / math.sqrt(HEAD_WIDTH)
    slot_ids = jnp.arange(capacity, dtype=jnp.int32)
    own_count = jnp.sum(
        jnp.where(jnp.arange(ctx_size, dtype=jnp.int32) == own_shard, valid_count, 0)
    )
    live_query = slot_ids < own_count
    query_pos = jnp.where(live_query, select_index, shard_len)
    key_shard = jnp.arange(all_keys, dtype=jnp.int32) // capacity
    key_live = (slot_ids[None, :] < valid_count[:, None]).reshape(all_keys)
    key_pos = jnp.tile(select_index, ctx_size)
    picked = jnp.take(tokens, select_index, axis=0)
    weight_key, weight_value = (
        lax.all_gather(key_matrix, "ctx", axis=0, tiled=True),
        lax.all_gather(value_matrix, "ctx", axis=0, tiled=True),
    )
    both_weights = jnp.concatenate([weight_key, weight_value], axis=1)
    projected = jnp.dot(picked, both_weights, preferred_element_type=jnp.float32).astype(
        jnp.bfloat16
    )
    kv_rows = lax.all_gather(projected, "ctx", axis=0, tiled=True)
    heads_of_query = queries.reshape(capacity, kv_local, per_group, HEAD_WIDTH)
    gradient_rows = jnp.where(live_query[:, None], out_grad, jnp.zeros_like(out_grad))
    gradient_heads = gradient_rows.reshape(capacity, kv_local, per_group, HEAD_WIDTH)
    stat_shape = (kv_local, per_group, capacity)

    def block_data(blk_id):
        leading_item = blk_id * block_len
        kv_blk = lax.dynamic_slice_in_dim(kv_rows, leading_item, block_len, 0)
        key_block = kv_blk[:, :key_value_width].reshape(block_len, kv_local, HEAD_WIDTH)
        value_block = kv_blk[:, key_value_width:].reshape(block_len, kv_local, HEAD_WIDTH)
        live_blk = lax.dynamic_slice_in_dim(key_live, leading_item, block_len, 0)
        shard_blk = lax.dynamic_slice_in_dim(key_shard, leading_item, block_len, 0)
        pos_blk = lax.dynamic_slice_in_dim(key_pos, leading_item, block_len, 0)
        same_shard = (shard_blk[None, :] == own_shard) & (pos_blk[None, :] <= query_pos[:, None])
        visible = live_blk[None, :] & ((shard_blk[None, :] < own_shard) | same_shard)
        active = leading_item // capacity <= own_shard
        return (key_block, value_block, visible, active)

    def block_scores(key_block, visible):
        scores = (
            jnp.einsum(
                "toul,iol->outi", heads_of_query, key_block, preferred_element_type=jnp.float32
            )
            * score_scale
        )
        return jnp.where(visible[None, None], scores, neg_large)

    def max_step(carried, blk_id):
        row_max, row_sum = carried
        key_block, value_block, visible, active = block_data(blk_id)

        def max_visit():
            scores = block_scores(key_block, visible)
            new_max = jnp.maximum(row_max, jnp.max(scores, axis=-1))
            terms = jnp.where(visible[None, None], jnp.exp(scores - new_max[..., None]), 0.0)
            new_sum = row_sum * jnp.exp(row_max - new_max) + jnp.sum(terms, axis=-1)
            return ((new_max, new_sum), scores)

        def max_ignore():
            return ((row_max, row_sum), jnp.full(stat_shape + (block_len,), neg_large, jnp.float32))

        stats, scores = lax.cond(active, max_visit, max_ignore)
        return (stats, None)

    start_stats = (jnp.full(stat_shape, neg_large, jnp.float32), jnp.zeros(stat_shape, jnp.float32))
    block_ids = jnp.arange(num_blocks, dtype=jnp.int32)
    (row_max, row_sum), stored = lax.scan(max_step, start_stats, block_ids)
    log_total = row_max + jnp.log(row_sum)

    def get_scores(key_block, visible):
        return block_scores(key_block, visible)

    def out_step(output_acc, blk_id):
        key_block, value_block, visible, active = block_data(blk_id)

        def out_visit():
            probs = jnp.exp(get_scores(key_block, visible) - log_total[..., None])
            weight_matrices = probs.astype(jnp.bfloat16)
            return output_acc + jnp.einsum(
                "ljvo,olf->vljf", weight_matrices, value_block, preferred_element_type=jnp.float32
            )

        def out_ignore():
            return output_acc

        return (lax.cond(active, out_visit, out_ignore), None)

    head_shape = (capacity, kv_local, per_group, HEAD_WIDTH)
    output_acc, unused = lax.scan(out_step, jnp.zeros(head_shape, jnp.float32), block_ids)
    attended = jnp.where(live_query[:, None, None, None], output_acc, 0.0).astype(jnp.bfloat16)
    out_dot = jnp.transpose(
        jnp.sum(gradient_heads.astype(jnp.float32) * attended.astype(jnp.float32), axis=-1),
        (1, 2, 0),
    )

    def grad_step(query_acc, blk_id):
        key_block, value_block, visible, active = block_data(blk_id)

        def grad_visit():
            probs = jnp.exp(get_scores(key_block, visible) - log_total[..., None])
            weight_matrices = probs.astype(jnp.bfloat16)
            grad_probs = jnp.einsum(
                "toul,iol->outi", gradient_heads, value_block, preferred_element_type=jnp.float32
            )
            score_gradient = (probs * (grad_probs - out_dot[..., None]) * score_scale).astype(
                jnp.bfloat16
            )
            new_acc = query_acc + jnp.einsum(
                "ljvo,olf->vljf", score_gradient, key_block, preferred_element_type=jnp.float32
            )
            key_part = jnp.einsum(
                "cifh,fcij->hcj", score_gradient, heads_of_query, preferred_element_type=jnp.float32
            )
            value_part = jnp.einsum(
                "cifh,fcij->hcj",
                weight_matrices,
                gradient_heads,
                preferred_element_type=jnp.float32,
            )
            return (
                new_acc,
                jnp.concatenate(
                    [
                        key_part.reshape(block_len, key_value_width),
                        value_part.reshape(block_len, key_value_width),
                    ],
                    axis=1,
                ),
            )

        def grad_ignore():
            return (query_acc, jnp.zeros((block_len, 2 * key_value_width), jnp.float32))

        return lax.cond(active, grad_visit, grad_ignore)

    query_acc, kv_terms = lax.scan(grad_step, jnp.zeros(head_shape, jnp.float32), block_ids)
    query_gradient = query_acc.astype(jnp.bfloat16).reshape(
        capacity, kv_local * per_group * HEAD_WIDTH
    )
    kv_terms = kv_terms.reshape(all_keys, 2 * key_value_width)
    own_grads = lax.psum_scatter(kv_terms, "ctx", scatter_dimension=0, tiled=True).astype(
        jnp.bfloat16
    )
    weight_grad = lax.psum_scatter(
        lax.dot_general(
            picked, own_grads, (((0,), (0,)), ((), ())), preferred_element_type=jnp.float32
        ),
        "ctx",
        scatter_dimension=0,
        tiled=True,
    )
    key_weight_grad = weight_grad[:, :key_value_width].astype(jnp.bfloat16)
    value_weight_grad = weight_grad[:, key_value_width:].astype(jnp.bfloat16)
    row_grad = lax.dot_general(
        own_grads, both_weights, (((1,), (1,)), ((), ())), preferred_element_type=jnp.float32
    )
    summed = lax.psum_scatter(row_grad, "tp", scatter_dimension=1, tiled=True)
    summed = jnp.where(live_query[:, None], summed, 0.0)
    token_grad = (
        jnp.zeros((shard_len, summed.shape[1]), jnp.float32)
        .at[select_index]
        .set(summed)
        .astype(jnp.bfloat16)
    )
    return (
        attended.reshape(capacity, kv_local * per_group * HEAD_WIDTH),
        query_gradient,
        token_grad,
        key_weight_grad,
        value_weight_grad,
    )


def solution(mesh):
    in_specs = (
        P("ctx", None),
        P("ctx"),
        P(),
        P("ctx", "tp"),
        P("ctx", "tp"),
        P("ctx", "tp"),
        P("ctx", "tp"),
    )
    out_specs = (P("ctx", "tp"), P("ctx", "tp"), P("ctx", "tp"), P("ctx", "tp"), P("ctx", "tp"))
    return jax.shard_map(local, mesh=mesh, in_specs=in_specs, out_specs=out_specs, check_vma=False)
```

profile of v0, /device:TPU:8, one launch (start us, length us, event | category | flops | bytes accessed | tf_op | source)
XLA Modules:
  0.0 1205.8 jit_solution(602995603653789307)
XLA Ops:
  7.2 0.7 all-gather.4.cloned.1.call-update
  7.9 0.7 all-gather.6.cloned.1.call-update
  8.7 1.3 fusion.76
  10.0 1.2 broadcast_select_fusion.3
  11.2 4.1 gather_fusion
  15.3 116.2 %all-gather.4.cloned.1.call-done = bf16[8192,128]{1,0:T(8,128)(2,1)} async-done(((bf16[128,128]{1,0:T(8,128)(2,1)}), bf16[8192,128]{1,0:T(8,128)(2,1)}) %all-gather.4.cloned.1.call-update) | async-done | bytes 2097168 | tf_op jit(solution)/shard_map/all_gather | solution.py:34
  131.5 3.2 constant_dynamic-update-slice_fusion.2
  134.7 114.9 %all-gather.6.cloned.1.call-done = bf16[8192,128]{1,0:T(8,128)(2,1)} async-done(((bf16[128,128]{1,0:T(8,128)(2,1)}), bf16[8192,128]{1,0:T(8,128)(2,1)}) %all-gather.6.cloned.1.call-update) | async-done | bytes 2097168 | tf_op jit(solution)/shard_map/all_gather | solution.py:35
  249.6 3.1 constant_dynamic-update-slice_fusion.1
  252.7 3.7 convolution_convert_fusion
  257.2 110.9 %all-gather.8.cloned.1.call-done = bf16[2048,256]{1,0:T(8,128)(2,1)} async-done(((bf16[32,256]{1,0:T(8,128)(2,1)}), bf16[2048,256]{1,0:T(8,128)(2,1)}) %all-gather.8.cloned.1.call-update) | async-done | bytes 1048592 | tf_op jit(solution)/shard_map/all_gather | solution.py:41
  368.1 7.5 while.49
  368.2 0.6 dynamic_slice.201
  369.5 2.1 conditional.9
  370.1 1.2 fusion.80
  371.6 0.6 dynamic_slice.201
  373.0 0.6 dynamic_slice.201
  374.3 0.6 dynamic_slice.201
  375.7 7.3 while.50
  375.7 0.6 dynamic_slice.202
  377.0 2.0 conditional.10
  377.6 1.4 fusion.31
  379.0 0.6 dynamic_slice.202
  380.3 0.6 dynamic_slice.202
  381.7 0.6 dynamic_slice.202
  383.3 14.4 %while.51 = (s32[]{:T(128)}, f32[32,1,8,128]{3,0,2,1:T(8,128)S(1)}, f32[4,512,256]{2,1,0:T(8,128)}, s32[4]{0:T(128)S(1)}, s32[]{:T(128)}, /*index=5*/bf16[2048,2...) while((s32[]{:T(128)}, f32[32,1,8,128]{3,0,2,1:T(8,128)S(1)}, ...), condition=%wide.region_15.16_spmd.clone, body=%wide.region_12.15_spmd.clone.sunk | while | flops 169058832 | bytes 7068294 | solution.py:157
  383.3 0.6 dynamic_slice.203
  384.6 4.7 conditional.11
  385.2 1.2 fusion.52
  386.4 1.2 fusion.53
  387.6 1.2 fusion.54
  389.5 0.8 constant_dynamic-update-slice_fusion.4
  390.4 0.6 dynamic_slice.203
  392.0 0.8 constant_dynamic-update-slice_fusion.4
  392.8 0.6 dynamic_slice.203
  394.4 0.9 constant_dynamic-update-slice_fusion.4
  395.3 0.6 dynamic_slice.203
  396.9 0.8 constant_dynamic-update-slice_fusion.4
  397.8 392.4 %reduce-scatter.4.cloned.1.call-done = f32[32,256]{1,0:T(8,128)} async-done(((f32[2048,256]{1,0:T(8,128)}), f32[32,256]{1,0:T(8,128)}) %reduce-scatter.4.cloned.1.call-update) | async-done | bytes 32784 | tf_op jit(solution)/shard_map/reduce_scatter | solution.py:162
  790.2 4.5 fusion.74
  794.8 4.6 fusion.69
  799.5 0.7 copy_bitcast_fusion
  800.2 9.3 reduce-scatter.6.cloned.1.call-done
  809.4 1.8 scatter_custom_fusion
  811.2 1.1 convert_element_type.73
  812.3 385.1 %reduce-scatter.8.cloned.1.call-done = f32[128,256]{1,0:T(8,128)} async-done(((f32[8192,256]{1,0:T(8,128)}), f32[128,256]{1,0:T(8,128)}) %reduce-scatter.8.cloned.1.call-update) | async-done | bytes 131088 | tf_op jit(solution)/shard_map/reduce_scatter | solution.py:165
  1197.4 0.9 convert.4
  1198.4 0.6 fusion.81
  (127 shorter events, 5.3 us)
Async XLA Ops:
  7.2 124.3 %all-gather.4.cloned.1.call-start = ((), (), s32[]{:S(2)}) async-start(), calls=%async_computation.3 | async-start | bytes 2129920 | tf_op jit(solution)/shard_map/all_gather | solution.py:34
  7.9 241.7 %all-gather.6.cloned.1.call-start = ((), (), s32[]{:S(2)}) async-start(), calls=%async_computation.4 | async-start | bytes 2129920 | tf_op jit(solution)/shard_map/all_gather | solution.py:35
  8.7 359.5 %all-gather.8.cloned.1.call-start = ((), (), s32[]{:S(2)}) async-start(), calls=%async_computation.5 | async-start | bytes 1064960 | tf_op jit(solution)/shard_map/all_gather | solution.py:41
  11.2 4.1 copy-start.1
  252.7 4.4 copy-start.3
  252.7 4.5 copy-start.4
  252.7 115.4 %copy-start.2 = (s32[64]{0:T(128)S(1)}, s32[64]{0:T(128)}, u32[]{:S(2)}) copy-start(s32[64]{0:T(128)} %param.21) | copy-start | bytes 772
  256.4 533.8 %reduce-scatter.4.cloned.1.call-start = ((), (), s32[]{:S(2)}) async-start(), calls=%async_computation.6 | async-start | bytes 2129920 | tf_op jit(solution)/shard_map/reduce_scatter | solution.py:162
  397.7 411.7 %reduce-scatter.6.cloned.1.call-start = ((), (), s32[]{:S(2)}) async-start(), calls=%async_computation.7 | async-start | bytes 1310720 | tf_op jit(solution)/shard_map/reduce_scatter | solution.py:178
  790.2 4.6 copy-start
  794.7 402.7 %reduce-scatter.8.cloned.1.call-start = ((), (), s32[]{:S(2)}) async-start(), calls=%async_computation.8 | async-start | bytes 8519680 | tf_op jit(solution)/shard_map/reduce_scatter | solution.py:165
Sparse Core Ops, SparseCore 0:
  11.6 119.8 all-gather.3
  135.1 114.4 all-gather.5
  256.5 111.5 all-gather.7
  397.9 392.2 reduce-scatter.3
  794.9 14.5 reduce-scatter.5
  811.8 385.5 reduce-scatter.7
where the time goes:
time: 1210 us
  waiting for transfers between devices  1130 us (93%)
  local copies, waits for them, and re-layouts  24.3 us (2%)
  matrix products  19.4 us (2%)
  between operations  14.3 us (1%)
    reduce_scatter x1, waiting for transfers between devices, local(): lax.psum_scatter(kv_terms, 'ctx', scatter_dimension=0, tiled=True)  392 us
    reduce_scatter x1, waiting for transfers between devices, local(): lax.psum_scatter(lax.dot_general(picked, own_grads, (((0,), (0,)), ((), (...  385 us
    all_gather x1, waiting for transfers between devices, local(): lax.all_gather(key_matrix, 'ctx', axis=0, tiled=True)  116 us
    all_gather x1, waiting for transfers between devices, local(): lax.all_gather(value_matrix, 'ctx', axis=0, tiled=True)  115 us
    all_gather x1, waiting for transfers between devices, local(): kv_rows = lax.all_gather(projected, 'ctx', axis=0, tiled=True)  111 us
  transfers between devices with their start and end apart: 6, of which 6 were waited for; matrix products, arithmetic and copies ran while one was open for 2% of the time, Pallas kernels for 0%

commit v1 on v0

--- a/solution.py
+++ b/solution.py
@@ -6,6 +6,11 @@
 
 HEAD_WIDTH = 128
 neg_large = -1e30
+
+
+def gather_over(x, axis, along):
+    sent = jnp.stack([x] * lax.axis_size(axis))
+    return jnp.concatenate(lax.all_to_all(sent, axis, 0, 0), axis=along)
 
 
 def local(tokens, select_index, valid_count, queries, key_matrix, value_matrix, out_grad):
@@ -32,7 +37,7 @@
     picked = jnp.take(tokens, select_index, axis=0)
     weight_key, weight_value = (
         lax.all_gather(key_matrix, "ctx", axis=0, tiled=True),
-        lax.all_gather(value_matrix, "ctx", axis=0, tiled=True),
+        gather_over(value_matrix, "ctx", 0),
     )
     both_weights = jnp.concatenate([weight_key, weight_value], axis=1)
     projected = jnp.dot(picked, both_weights, preferred_element_type=jnp.float32).astype(

time: 1210 us -> 1100 us (0.909)
  waiting for transfers between devices: 1130 us -> 1020 us
  starting transfers between devices: 0.24 us -> 14.3 us
    all_gather x1 -> x0, waiting for transfers between devices: 115 us -> none  [local(): lax.all_gather(value_matrix, 'ctx', axis=0, tiled=True)]
    all_to_all x0 -> x1, waiting for transfers between devices: none -> 47.3 us  [gather_over(): return jnp.concatenate(lax.all_to_all(sent, axis, 0, 0), axis=along)]
    all_gather x1, waiting for transfers between devices: 116 us -> 70.2 us  [local(): lax.all_gather(key_matrix, 'ctx', axis=0, tiled=True)]
    all_to_all x0 -> x1, starting transfers between devices: none -> 14.1 us  [gather_over(): return jnp.concatenate(lax.all_to_all(sent, axis, 0, 0), axis=along)]
  transfers between devices with their start and end apart: 6 -> 6, of which waited for: 6 -> 6; matrix products, arithmetic and copies ran while one was open for 2% -> 1% of each run, Pallas kernels for 0% -> 0%
where the time goes in v1:
time: 1100 us
  waiting for transfers between devices  1020 us (93%)
  local copies, waits for them, and re-layouts  20.6 us (2%)
  matrix products  19.5 us (2%)
  starting transfers between devices  14.3 us (1%)
  between operations  14 us (1%)
    reduce_scatter x1, waiting for transfers between devices, local(): lax.psum_scatter(kv_terms, 'ctx', scatter_dimension=0, tiled=True)  392 us
    reduce_scatter x1, waiting for transfers between devices, local(): lax.psum_scatter(lax.dot_general(picked, own_grads, (((0,), (0,)), ((), (...  385 us
    all_gather x1, waiting for transfers between devices, local(): kv_rows = lax.all_gather(projected, 'ctx', axis=0, tiled=True)  111 us
    all_gather x1, waiting for transfers between devices, local(): lax.all_gather(key_matrix, 'ctx', axis=0, tiled=True)  70.2 us
    all_to_all x1, waiting for transfers between devices, gather_over(): return jnp.concatenate(lax.all_to_all(sent, axis, 0, 0), axis=along)  47.3 us
  transfers between devices with their start and end apart: 6, of which 6 were waited for; matrix products, arithmetic and copies ran while one was open for 1% of the time, Pallas kernels for 0%

profile of v1, /device:TPU:8, one launch (start us, length us, event | category | flops | bytes accessed | tf_op | source)
XLA Modules:
  0.0 1100.1 jit_solution(16934943257048562452)
XLA Ops:
  7.2 2.6 stack.2
  9.8 14.1 %all-to-all-start = ((bf16[64,128,128]{2,1,0:T(8,128)(2,1)}), bf16[64,128,128]{2,1,0:T(8,128)(2,1)}, u32[]{:S(2)}, u32[]{:S(2)}) async-start(bf16[64,128,128]{2,1,0:T(8,128)(2,1)} %stack.2), calls=%async_computation | async-start | bytes 4194304 | tf_op jit(solution)/shard_map/all_to_all | solution.py:13
  23.9 0.7 all-gather.3.cloned.1.call-update
  24.7 0.7 fusion.78
  25.3 0.6 broadcast_select_fusion.3
  26.0 4.1 gather_fusion
  30.1 47.3 %all-to-all-done = bf16[64,128,128]{2,1,0:T(8,128)(2,1)} async-done(((bf16[64,128,128]{2,1,0:T(8,128)(2,1)}), bf16[64,128,128]{2,1,0:T(8,128)(2,1)}, u32[]{:S(2)}, u32[]{:S(2)}) %all-to-all-start) | async-done | bytes 2097184 | tf_op jit(solution)/shard_map/all_to_all | solution.py:13
  77.4 70.2 %all-gather.3.cloned.1.call-done = bf16[8192,128]{1,0:T(8,128)(2,1)} async-done(((bf16[128,128]{1,0:T(8,128)(2,1)}), bf16[8192,128]{1,0:T(8,128)(2,1)}) %all-gather.3.cloned.1.call-update) | async-done | bytes 2097168 | tf_op jit(solution)/shard_map/all_gather | solution.py:39
  147.7 3.7 fusion.68
  151.5 0.6 iota_compare_fusion
  152.3 111.1 %all-gather.5.cloned.1.call-done = bf16[2048,256]{1,0:T(8,128)(2,1)} async-done(((bf16[32,256]{1,0:T(8,128)(2,1)}), bf16[2048,256]{1,0:T(8,128)(2,1)}) %all-gather.5.cloned.1.call-update) | async-done | bytes 1048592 | tf_op jit(solution)/shard_map/all_gather | solution.py:46
  263.4 7.4 while.49
  263.4 0.6 dynamic_slice.201
  264.7 2.1 conditional.9
  265.4 1.2 fusion.84
  266.9 0.6 dynamic_slice.201
  268.2 0.6 dynamic_slice.201
  269.6 0.6 dynamic_slice.201
  270.9 7.3 while.50
  271.0 0.6 dynamic_slice.202
  272.3 2.0 conditional.10
  272.9 1.4 fusion.31
  274.3 0.6 dynamic_slice.202
  275.6 0.6 dynamic_slice.202
  276.9 0.6 dynamic_slice.202
  278.6 14.4 %while.51 = (s32[]{:T(128)}, f32[32,1,8,128]{3,0,2,1:T(8,128)S(1)}, f32[4,512,256]{2,1,0:T(8,128)}, s32[4]{0:T(128)S(1)}, s32[]{:T(128)}, /*index=5*/bf16[2048,2...) while((s32[]{:T(128)}, f32[32,1,8,128]{3,0,2,1:T(8,128)S(1)}, ...), condition=%wide.region_15.16_spmd.clone, body=%wide.region_12.15_spmd.clone.sunk | while | flops 169058832 | bytes 7068294 | solution.py:162
  278.6 0.6 dynamic_slice.203
  279.9 4.7 conditional.11
  280.5 1.2 fusion.52
  281.7 1.2 fusion.53
  282.9 1.2 fusion.54
  284.8 0.8 constant_dynamic-update-slice_fusion.2
  285.6 0.6 dynamic_slice.203
  287.2 0.9 constant_dynamic-update-slice_fusion.2
  288.1 0.6 dynamic_slice.203
  289.7 0.9 constant_dynamic-update-slice_fusion.2
  290.5 0.6 dynamic_slice.203
  292.1 0.9 constant_dynamic-update-slice_fusion.2
  293.0 392.3 %reduce-scatter.4.cloned.1.call-done = f32[32,256]{1,0:T(8,128)} async-done(((f32[2048,256]{1,0:T(8,128)}), f32[32,256]{1,0:T(8,128)}) %reduce-scatter.4.cloned.1.call-update) | async-done | bytes 32784 | tf_op jit(solution)/shard_map/reduce_scatter | solution.py:167
  685.3 4.5 fusion.66
  690.0 4.6 fusion.72
  694.7 0.7 copy_bitcast_fusion
  695.3 9.1 reduce-scatter.6.cloned.1.call-done
  704.5 1.8 scatter_custom_fusion
  706.2 1.1 convert_element_type.73
  707.4 384.6 %reduce-scatter.8.cloned.1.call-done = f32[128,256]{1,0:T(8,128)} async-done(((f32[8192,256]{1,0:T(8,128)}), f32[128,256]{1,0:T(8,128)}) %reduce-scatter.8.cloned.1.call-update) | async-done | bytes 131088 | tf_op jit(solution)/shard_map/reduce_scatter | solution.py:170
  1092.0 0.9 convert.4
  1092.9 0.6 fusion.85
  (125 shorter events, 4.7 us)
Async XLA Ops:
  9.8 14.9 %copy-start.1 = (s32[64]{0:T(128)S(1)}, s32[64]{0:T(128)}, u32[]{:S(2)}) copy-start(s32[64]{0:T(128)} %param.21) | copy-start | bytes 772
  9.8 15.5 %copy-start = (s32[32]{0:T(128)S(1)}, s32[32]{0:T(128)}, u32[]{:S(2)}) copy-start(s32[32]{0:T(128)} %param.20) | copy-start | bytes 388
  9.8 67.6 %all-to-all-start = ((bf16[64,128,128]{2,1,0:T(8,128)(2,1)}), bf16[64,128,128]{2,1,0:T(8,128)(2,1)}, u32[]{:S(2)}, u32[]{:S(2)}) async-start(bf16[64,128,128]{2,1,0:T(8,128)(2,1)} %stack.2), calls=%async_computation | async-start | bytes 4194304 | tf_op jit(solution)/shard_map/all_to_all | solution.py:13
  23.9 123.8 %all-gather.3.cloned.1.call-start = ((), (), s32[]{:S(2)}) async-start(), calls=%async_computation.4 | async-start | bytes 2129920 | tf_op jit(solution)/shard_map/all_gather | solution.py:39
  24.6 238.8 %all-gather.5.cloned.1.call-start = ((), (), s32[]{:S(2)}) async-start(), calls=%async_computation.5 | async-start | bytes 1064960 | tf_op jit(solution)/shard_map/all_gather | solution.py:46
  147.7 3.8 copy-start.2
  147.7 4.5 copy-start.3
  151.4 533.9 %reduce-scatter.4.cloned.1.call-start = ((), (), s32[]{:S(2)}) async-start(), calls=%async_computation.6 | async-start | bytes 2129920 | tf_op jit(solution)/shard_map/reduce_scatter | solution.py:167
  293.0 411.5 %reduce-scatter.6.cloned.1.call-start = ((), (), s32[]{:S(2)}) async-start(), calls=%async_computation.7 | async-start | bytes 1310720 | tf_op jit(solution)/shard_map/reduce_scatter | solution.py:183
  685.3 4.6 copy-start.4
  689.9 402.1 %reduce-scatter.8.cloned.1.call-start = ((), (), s32[]{:S(2)}) async-start(), calls=%async_computation.8 | async-start | bytes 8519680 | tf_op jit(solution)/shard_map/reduce_scatter | solution.py:170
Sparse Core Ops, SparseCore 0:
  28.3 119.3 all-gather.2
  151.9 111.5 all-gather.4
  293.1 392.1 reduce-scatter.3
  690.0 14.3 reduce-scatter.5
  706.9 385.0 reduce-scatter.7
